TPU v7x, 32 devices: a whole 2x2x4 slice. The times are simulated.
32 devices in a mesh: tensor: 4 (over z), tokens: 8 (over y, x, core).
Axes of the slice: x: 2, y: 2, z: 4, core: 2. Of those that a mesh axis runs over, the one named last changes fastest.
Arguments:
- hidden: bfloat16 [2048, 8192], P('tokens', 'tensor'), may hold values from -24 to 24
- w_query: bfloat16 [8192, 4096], P(None, 'tensor'), may hold values from -0.0625 to 0.0625
- w_key: bfloat16 [8192, 512], P(None, 'tensor'), may hold values from -0.0625 to 0.0625
- w_value: bfloat16 [8192, 512], P(None, 'tensor'), may hold values from -0.0625 to 0.0625
- key_codes: int32 [2048, 512], P('tokens', 'tensor'), may hold values from 0 to 15
- codebook: float32 [512, 16], P('tensor'), may hold values from -24 to 24
- positions: int32 [2048], P('tokens'), may hold values from 0 to 1535, as said below
- cotangent: bfloat16 [2048, 4096], P('tokens', 'tensor'), may hold values from -6 to 6
Outputs:
- attention_out: bfloat16 [2048, 4096], P('tokens', 'tensor')
- codebook_grad: float32 [512, 16], P('tensor')
Inputs may be any that keep to these rules, and one draw needn't show every extreme that they name: positions are 0 at the first token of each packed document and rise by one within it; exactly one document has 1536 tokens and every other is shorter.
All inputs are finite; a program needn't handle non-finite values.
Results may differ from a plain program's by a relative error of at most 0.0095.
The roundings to bfloat16 on the way count: a program that leaves them out, or rounds other values in their place, can miss the bound.
Values may be sent and summed in bfloat16 or wider, within the bound.
A program may use at most 128 MiB of HBM per device.

v0:
```python
import functools
import math

import jax
import jax.numpy as jnp
from jax import lax
from jax.experimental import pallas as pl
from jax.experimental.pallas import tpu as pltpu
from jax.sharding import PartitionSpec as P

HD = 128
ROPE_BASE = 500000.0
NEG_BIG = -1e30
SUBS = 4
MESH = pl.DeviceIdType.MESH


def trig_table(positions, width):
    index = jnp.arange(width // 2).astype(jnp.float32)
    inverse = jnp.exp(index * (-2.0 * math.log(ROPE_BASE) / width))
    angle = positions.astype(jnp.float32)[:, None] * jnp.tile(inverse, 2)[None, :]
    low = jnp.arange(width) < width // 2
    return jnp.where(low[None, :], jnp.cos(angle), jnp.sin(angle))


def split_trig(table):
    low = lax.broadcasted_iota(jnp.int32, table.shape, 1) < HD // 2
    rolled = pltpu.roll(table, HD // 2, 1)
    return jnp.where(low, table, rolled), jnp.where(low, -rolled, table)


def dot_nt(a, b):
    return lax.dot_general(a, b, (((1,), (1,)), ((), ())), preferred_element_type=jnp.float32)


def kernel(
    n_t, n_d, heads,
    x_hbm, wq_hbm, wk_hbm, wv_hbm, codes_hbm, trig_hbm, cbt, pos, cot,
    out_ref, grad_ref,
    xbuf, w, acc, codes, trig, kall, vall, vt, qst, dost, dot_t, probs, scores, dkey, bins, red, poss, outs,
    xsend, xrecv, xlocal, wsem, csend, crecv, clocal, ksend, krecv, vsend, vrecv, rsend, rrecv,
):
    subs, tile, feats = x_hbm.shape
    cols = heads * tile
    rows = subs * tile
    group = n_d * tile
    total = subs * group
    levels = cbt.shape[0]
    kb = min(256, group)
    per = kb // tile
    qw = heads * HD
    scale = 1.0 / math.sqrt(HD)
    shift = tile.bit_length() - 1
    z = lax.axis_index("tensor")
    d = lax.axis_index("tokens")
    has_left, has_right = z > 0, z < n_t - 1

    barrier = pltpu.get_barrier_semaphore()

    @pl.when(has_left)
    def _():
        pl.semaphore_signal(barrier, inc=1, device_id={"tensor": z - 1}, device_id_type=MESH)

    @pl.when(has_right)
    def _():
        pl.semaphore_signal(barrier, inc=1, device_id={"tensor": z + 1}, device_id_type=MESH)

    for k in range(1, n_d):
        pl.semaphore_signal(
            barrier, inc=1, device_id={"tokens": lax.rem(d + k, n_d)}, device_id_type=MESH
        )

    w_copies = [
        pltpu.make_async_copy(wq_hbm, w.at[:, pl.ds(0, qw)], wsem.at[0]),
        pltpu.make_async_copy(wk_hbm, w.at[:, pl.ds(qw, HD)], wsem.at[1]),
        pltpu.make_async_copy(wv_hbm, w.at[:, pl.ds(qw + HD, HD)], wsem.at[2]),
    ]
    x_own = pltpu.make_async_copy(x_hbm, xbuf.at[:, z], xlocal)
    c_own = pltpu.make_async_copy(codes_hbm, codes.at[:, d], clocal.at[0])
    t_own = pltpu.make_async_copy(trig_hbm, trig.at[:, d], clocal.at[1])

    pl.semaphore_wait(
        barrier, n_d - 1 + has_left.astype(jnp.int32) + has_right.astype(jnp.int32)
    )

    def own_hop(s, side):
        return pltpu.make_async_remote_copy(
            src_ref=x_hbm.at[s], dst_ref=xbuf.at[s, z],
            send_sem=xsend.at[side, s, z], recv_sem=xrecv.at[s, z],
            device_id={"tensor": z + 2 * side - 1}, device_id_type=MESH,
        )

    def hop(s, src, side):
        return pltpu.make_async_remote_copy(
            src_ref=xbuf.at[s, src], dst_ref=xbuf.at[s, src],
            send_sem=xsend.at[side, s, src], recv_sem=xrecv.at[s, src],
            device_id={"tensor": z + 2 * side - 1}, device_id_type=MESH,
        )

    def send_own(s):
        @pl.when(has_right)
        def _():
            own_hop(s, 1).start()

        @pl.when(has_left)
        def _():
            own_hop(s, 0).start()

    send_own(0)
    x_own.start()
    for copy in w_copies:
        copy.start()
    c_own.start()
    t_own.start()

    def key_copies(k, src):
        peer = {"tokens": lax.rem(d + k, n_d)}
        return [
            pltpu.make_async_remote_copy(
                src_ref=codes_hbm, dst_ref=codes.at[:, src],
                send_sem=csend.at[0, k], recv_sem=crecv.at[0, k],
                device_id=peer, device_id_type=MESH,
            ),
            pltpu.make_async_remote_copy(
                src_ref=trig_hbm, dst_ref=trig.at[:, src],
                send_sem=csend.at[1, k], recv_sem=crecv.at[1, k],
                device_id=peer, device_id_type=MESH,
            ),
        ]

    def dequantize(code):
        value = jnp.zeros(code.shape, jnp.float32)
        for level in range(levels):
            value = jnp.where(code == level, cbt[level:level + 1, :], value)
        return value

    c_own.wait()
    t_own.wait()
    for s in range(subs):
        cosine, sine = split_trig(trig[s, d])
        value = dequantize(codes[s, d])
        turned = value * cosine + pltpu.roll(value, HD // 2, 1) * sine
        kall[s, d] = turned.astype(jnp.bfloat16)

    low = lax.broadcasted_iota(jnp.int32, (8, HD), 1) < tile
    for s in range(subs):
        at = s * tile // HD * HD
        here = jnp.broadcast_to(pos[:, at:at + HD], (8, HD))
        other = pltpu.roll(here, tile, 1)
        twice = jnp.where(low, here, other) if s * tile % HD == 0 else jnp.where(low, other, here)
        poss[s] = jnp.concatenate([twice] * (cols // HD), axis=1)
    bins[...] = jnp.zeros_like(bins)
    outs[...] = jnp.zeros_like(outs)

    for s in range(subs):
        for h in range(heads):
            piece = cot[s * tile:(s + 1) * tile, h * HD:(h + 1) * HD]
            dost[s, h * tile:(h + 1) * tile, :] = piece
        dot_t[s] = dost[s].astype(jnp.float32).T

    def rot_copy(k):
        return pltpu.make_async_remote_copy(
            src_ref=kall.at[:, d], dst_ref=kall.at[:, d],
            send_sem=ksend.at[k], recv_sem=krecv.at[k],
            device_id={"tokens": lax.rem(d + k, n_d)}, device_id_type=MESH,
        )

    for k in range(1, n_d):
        rot_copy(k).start()
    for k in range(1, n_d):
        for copy in key_copies(k, d):
            copy.start()

    def add_bins(code, value):
        for level in range(levels):
            chosen = jnp.where(code == level, value, 0.0)
            bins[level] += jnp.sum(chosen.reshape(-1, 8, HD), axis=0)

    def block_at(b):
        start = b * kb
        s = start // group
        return s, (start - s * group) // tile

    x_own.wait()
    for copy in w_copies:
        copy.wait()

    def v_copy(s, k):
        mine = pl.ds(pl.multiple_of((s * n_d + d) * tile, tile), tile)
        return pltpu.make_async_remote_copy(
            src_ref=vall.at[mine], dst_ref=vall.at[mine],
            send_sem=vsend.at[s, k], recv_sem=vrecv.at[s, k],
            device_id={"tokens": lax.rem(d + k, n_d)}, device_id_type=MESH,
        )

    def take_values(c):
        for k in range(1, n_d):
            v_copy(c, k).wait_recv()
        block = vall[pl.ds(pl.multiple_of(c * group, group), group), :]
        vt[c] = block.astype(jnp.float32).T.astype(jnp.bfloat16)

    def add_out(s, c):
        part = probs[s, pl.ds(pl.multiple_of(c * group, group), group), :]
        outs[s] += jnp.dot(vt[c], part, preferred_element_type=jnp.float32)

    def sub(s, carry):
        @pl.when(s + 1 < subs)
        def _():
            send_own(s + 1)

        acc[...] = jnp.zeros_like(acc)

        def multiply(src):
            part = w[pl.ds(pl.multiple_of(src * feats, feats), feats), :]
            acc[...] += jnp.dot(xbuf[s, src], part, preferred_element_type=jnp.float32)

        def step(k, inner):
            from_left = z - k
            from_right = z + k
            left_on = (k > 0) & (from_left >= 0)
            right_on = (k > 0) & (from_right < n_t)

            @pl.when(left_on)
            def _():
                hop(s, from_left, 1).wait_recv()

                @pl.when(has_right)
                def _():
                    hop(s, from_left, 1).start()

            @pl.when(from_left >= 0)
            def _():
                multiply(from_left)

            @pl.when(right_on)
            def _():
                hop(s, from_right, 0).wait_recv()

                @pl.when(has_left)
                def _():
                    hop(s, from_right, 0).start()

                multiply(from_right)

            return inner

        lax.fori_loop(0, n_t, step, 0)
        mine = pl.ds(pl.multiple_of((s * n_d + d) * tile, tile), tile)
        vall[mine, :] = acc[:, qw + HD:qw + 2 * HD].astype(jnp.bfloat16)

        @pl.when(s == 0)
        def _():
            for k in range(1, n_d):
                rot_copy(k).wait_recv()

        cosine, sine = split_trig(trig[s, d])
        for h in range(heads):
            value = acc[:, h * HD:(h + 1) * HD]
            turned = value * cosine + pltpu.roll(value, HD // 2, 1) * sine
            qst[s, h * tile:(h + 1) * tile, :] = turned.astype(jnp.bfloat16)
        for k in range(1, n_d):
            v_copy(s, k).start()
        code = codes[s, d]
        add_bins(code, (levels / total) * (dequantize(code) - acc[:, qw:qw + HD]))

        column = lax.broadcasted_iota(jnp.int32, (1, cols), 1)
        query = d * rows + s * tile + (column & (tile - 1))
        earliest = query - poss[s, 0:1, :]
        q = qst[s]

        def score(b, peak):
            sk, first = block_at(b)
            at = pl.ds(pl.multiple_of(b * kb, kb), kb)
            row = lax.broadcasted_iota(jnp.int32, (kb, 1), 0)
            key = ((row >> shift) + first) * rows + sk * tile + (row & (tile - 1))
            value = dot_nt(kall[sk, pl.ds(first, per)].reshape(kb, HD), q) * scale
            value = jnp.where((key <= query) & (key >= earliest), value, NEG_BIG)
            scores[at, :] = value
            return jnp.maximum(peak, jnp.max(value, axis=0, keepdims=True))

        peak = lax.fori_loop(
            0, total // kb, score, jnp.full((1, cols), NEG_BIG, jnp.float32)
        )

        def exponent(b, mass):
            at = pl.ds(pl.multiple_of(b * kb, kb), kb)
            value = jnp.exp(scores[at, :] - peak)
            scores[at, :] = value
            return mass + jnp.sum(value, axis=0, keepdims=True)

        mass = lax.fori_loop(0, total // kb, exponent, jnp.zeros((1, cols), jnp.float32))
        inverse = 1.0 / mass

        def normal(b, inner):
            at = pl.ds(pl.multiple_of(b * kb, kb), kb)
            probs[s, at, :] = (scores[at, :] * inverse).astype(jnp.bfloat16)
            return inner

        lax.fori_loop(0, total // kb, normal, 0)

        @pl.when(s > 0)
        def _():
            take_values(s - 1)

            def older(c, inner):
                add_out(s, c)
                return inner

            def newest(q_at, inner):
                add_out(q_at, s - 1)
                return inner

            lax.fori_loop(0, s, older, 0)
            lax.fori_loop(0, s, newest, 0)

        return carry

    lax.fori_loop(0, subs, sub, 0)
    take_values(subs - 1)

    dkey[...] = jnp.zeros_like(dkey)

    def tail(s, carry):
        add_out(s, subs - 1)
        output = outs[s].astype(jnp.bfloat16).astype(jnp.float32)
        delta = jnp.sum(output * dot_t[s], axis=0, keepdims=True)
        output = output.T.astype(jnp.bfloat16)
        for h in range(heads):
            out_ref[pl.ds(pl.multiple_of(s * tile, tile), tile), h * HD:(h + 1) * HD] = output[
                h * tile:(h + 1) * tile, :
            ]
        grad_out = dost[s]
        q = qst[s]

        def block(b, inner):
            at = pl.ds(pl.multiple_of(b * kb, kb), kb)
            dprobs = dot_nt(vall[at, :], grad_out)
            dscores = (probs[s, at, :].astype(jnp.float32) * (dprobs - delta)).astype(jnp.bfloat16)
            dkey[at, :] += jnp.dot(dscores, q, preferred_element_type=jnp.float32)
            return inner

        return lax.fori_loop(0, total // kb, block, carry, unroll=4)

    lax.fori_loop(0, subs, tail, 0)

    def gather_bins(b, carry):
        s, first = block_at(b)
        code = codes[s, pl.ds(first, per)].reshape(kb, HD)
        cosine, sine = split_trig(trig[s, pl.ds(first, per)].reshape(kb, HD))
        grad = dkey[pl.ds(pl.multiple_of(b * kb, kb), kb), :] * scale
        add_bins(code, grad * cosine - pltpu.roll(grad, HD // 2, 1) * sine)
        return carry

    for k in range(1, n_d):
        for copy in key_copies(k, d):
            copy.wait_recv()
    lax.fori_loop(0, total // kb, gather_bins, 0)
    red[d] = jnp.sum(bins[...], axis=1)

    def x_drain(s, carry):
        def one(src, inner):
            @pl.when(has_right & (src <= z))
            def _():
                hop(s, src, 1).wait_send()

            @pl.when(has_left & (src >= z))
            def _():
                hop(s, src, 0).wait_send()

            return inner

        lax.fori_loop(0, n_t, one, 0)
        for k in range(1, n_d):
            v_copy(s, k).wait_send()
        return carry

    lax.fori_loop(0, subs, x_drain, 0)
    for k in range(1, n_d):
        rot_copy(k).wait_send()
        for copy in key_copies(k, d):
            copy.wait_send()

    sums = [
        pltpu.make_async_remote_copy(
            src_ref=red.at[d], dst_ref=red.at[d],
            send_sem=rsend.at[k], recv_sem=rrecv.at[k],
            device_id={"tokens": lax.rem(d + k, n_d)}, device_id_type=MESH,
        )
        for k in range(1, n_d)
    ]
    for copy in sums:
        copy.start()
    for copy in sums:
        copy.wait()
    grad_ref[...] = jnp.sum(red[...], axis=0)


def shards(hidden, w_query, w_key, w_value, key_codes, codebook, positions, cotangent):
    rows, feats = hidden.shape
    width = w_query.shape[0]
    heads = w_query.shape[1] // HD
    levels = codebook.shape[1]
    n_t, n_d = lax.axis_size("tensor"), lax.axis_size("tokens")
    subs, tile = SUBS, rows // SUBS
    cols, total = heads * tile, rows * n_d
    trig = trig_table(positions, HD).reshape(subs, tile, HD)
    pos = positions.reshape(1, rows)
    anywhere = pl.BlockSpec(memory_space=pl.ANY)
    vmem = pl.BlockSpec(memory_space=pltpu.VMEM)
    dma = pltpu.SemaphoreType.DMA
    bf16, f32 = jnp.bfloat16, jnp.float32
    out, grad = pl.pallas_call(
        functools.partial(kernel, n_t, n_d, heads),
        out_shape=(
            jax.ShapeDtypeStruct((rows, heads * HD), bf16),
            jax.ShapeDtypeStruct((levels, HD), f32),
        ),
        in_specs=[anywhere] * 6 + [vmem] * 3,
        out_specs=(vmem, vmem),
        scratch_shapes=[
            pltpu.VMEM((subs, n_t, tile, feats), bf16),
            pltpu.VMEM((width, heads * HD + 2 * HD), bf16),
            pltpu.VMEM((tile, heads * HD + 2 * HD), f32),
            pltpu.VMEM((subs, n_d, tile, HD), jnp.int32),
            pltpu.VMEM((subs, n_d, tile, HD), f32),
            pltpu.VMEM((subs, n_d, tile, HD), bf16),
            pltpu.VMEM((total, HD), bf16),
            pltpu.VMEM((subs, HD, n_d * tile), bf16),
            pltpu.VMEM((subs, cols, HD), bf16),
            pltpu.VMEM((subs, cols, HD), bf16),
            pltpu.VMEM((subs, HD, cols), f32),
            pltpu.VMEM((subs, total, cols), bf16),
            pltpu.VMEM((total, cols), f32),
            pltpu.VMEM((total, HD), f32),
            pltpu.VMEM((levels, 8, HD), f32),
            pltpu.VMEM((n_d, levels, HD), f32),
            pltpu.VMEM((subs, 8, cols), jnp.int32),
            pltpu.VMEM((subs, HD, cols), f32),
            dma((2, subs, n_t)),
            dma((subs, n_t)),
            dma,
            dma((3,)),
            dma((2, n_d)),
            dma((2, n_d)),
            dma((2,)),
            dma((n_d,)),
            dma((n_d,)),
            dma((subs, n_d)),
            dma((subs, n_d)),
            dma((n_d,)),
            dma((n_d,)),
        ],
        compiler_params=pltpu.CompilerParams(
            collective_id=0, has_side_effects=True, vmem_limit_bytes=67043328
        ),
    )(
        hidden.reshape(subs, tile, feats), w_query, w_key, w_value,
        key_codes.reshape(subs, tile, HD), trig, codebook.T, pos, cotangent,
    )
    return out, grad.T


def solution(mesh):
    placed = (
        P("tokens", "tensor"),
        P(None, "tensor"),
        P(None, "tensor"),
        P(None, "tensor"),
        P("tokens", "tensor"),
        P("tensor", None),
        P("tokens"),
        P("tokens", "tensor"),
    )
    return jax.shard_map(
        shards,
        mesh=mesh,
        in_specs=placed,
        out_specs=(P("tokens", "tensor"), P("tensor", None)),
        check_vma=False,
    )
```

profile of v0, /device:TPU:0, one launch (start us, length us, event | category | flops | bytes accessed | tf_op | source)
XLA Modules:
  0.0 110.0 jit_solution(13252746690006585141)
XLA Ops:
  0.7 0.1 mul.32
  0.7 0.7 convert_element_type.10
  1.4 0.1 mul.28
  1.5 1.2 %fusion.trig_hbm = f32[4,64,128]{2,1,0:T(8,128)} fusion(f32[128]{0:T(128)S(1)} %mul.32, f32[4,64]{1,0:T(4,128)S(1)} %mul.28, pred[128]{0:T(512)(128)(4,1)S(1)} %iota_compare_fusion), kind=kLoop, calls=%fused_computation.2 | loop fusion | flops 65536 | bytes 132736 | tf_op jit(solution)/shard_map/jit(_where)/select_n | solution.py:23
  2.7 104.1 %shard_map.95 = (bf16[256,1024]{1,0:T(8,128)(2,1)}, f32[16,128]{1,0:T(8,128)}) custom-call(bf16[4,64,2048]{2,1,0:T(8,128)(2,1)} %bitcast.5, bf16[8192,1024]{1,0:T(8,128)(2,1)} %wq_hbm.1, bf16[8192,128]{1,0:T(8,128)(2,1)} %wk_hbm.1, bf16[8192,128]{1,0:T(8,128)(2,1)} %wv_hbm.1, s32[4,64,128]{2,1,0:T(8,128)} %bitcast.6, f32[4,64,128]{2,1,0:T(8,128)} %fusion.trig_hbm, ...), custom_call_target="tpu_custom_call" | custom-call | tf_op jit(solution)/shard_map/pallas_call | solution.py:412
  106.8 1.9 %copy.12 = bf16[256,1024]{1,0:T(8,128)(2,1)} copy(bf16[256,1024]{1,0:T(8,128)(2,1)} %get-tuple-element.8) | data formatting | bytes 1048576
  108.7 1.3 %copy.13 = f32[128,16]{0,1:T(8,128)} copy(f32[128,16]{0,1:T(8,128)} %bitcast.8) | data formatting | bytes 16384
  (3 shorter events, 0.0 us)
where the time goes:
time: 110 us
  Pallas kernels  104 us (95%)
  local copies, waits for them, and re-layouts  3.33 us (3%)
  other arithmetic  1.89 us (2%)
    pallas_call x1, Pallas kernels, shards(): pl.pallas_call(functools.partial(kernel, n_t, n_d, heads), out_shape=(jax...  104 us
    unnamed x2, local copies, waits for them, and re-layouts  3.16 us

commit v1 on v0

v1 whole, which is shorter than its diff:
```python
import functools
import math

import jax
import jax.numpy as jnp
from jax import lax
from jax.experimental import pallas as pl
from jax.experimental.pallas import tpu as pltpu
from jax.sharding import PartitionSpec as P

HD = 128
ROPE_BASE = 500000.0
NEG_BIG = -1e30
SUBS = 4
MESH = pl.DeviceIdType.MESH


def trig_table(positions, width):
    index = jnp.arange(width // 2).astype(jnp.float32)
    inverse = jnp.exp(index * (-2.0 * math.log(ROPE_BASE) / width))
    angle = positions.astype(jnp.float32)[:, None] * jnp.tile(inverse, 2)[None, :]
    low = jnp.arange(width) < width // 2
    return jnp.where(low[None, :], jnp.cos(angle), jnp.sin(angle))


def split_trig(table):
    low = lax.broadcasted_iota(jnp.int32, table.shape, 1) < HD // 2
    rolled = pltpu.roll(table, HD // 2, 1)
    return jnp.where(low, table, rolled), jnp.where(low, -rolled, table)


def dot_nt(a, b):
    return lax.dot_general(a, b, (((1,), (1,)), ((), ())), preferred_element_type=jnp.float32)


def kernel(
    n_t, n_d, heads,
    x_hbm, wq_hbm, wk_hbm, wv_hbm, codes_hbm, trig_hbm, cbt, pos, cot,
    out_ref, grad_ref,
    xbuf, w, acc, codes, trig, kall, vall, vt, qst, dost, dot_t, probs, scores, deltas, bins, red, poss, outs,
    xsend, xrecv, xlocal, wsem, csend, crecv, clocal, ksend, krecv, vsend, vrecv, rsend, rrecv,
):
    subs, tile, feats = x_hbm.shape
    cols = heads * tile
    rows = subs * tile
    total = rows * n_d
    levels = cbt.shape[0]
    qw = heads * HD
    width = qw + 2 * HD
    scale = 1.0 / math.sqrt(HD)
    longest = 3 * total // 4
    z = lax.axis_index("tensor")
    d = lax.axis_index("tokens")
    has_left, has_right = z > 0, z < n_t - 1
    first = jnp.maximum(d - longest // rows, 0)
    last = d + 1

    barrier = pltpu.get_barrier_semaphore()

    @pl.when(has_left)
    def _():
        pl.semaphore_signal(barrier, inc=1, device_id={"tensor": z - 1}, device_id_type=MESH)

    @pl.when(has_right)
    def _():
        pl.semaphore_signal(barrier, inc=1, device_id={"tensor": z + 1}, device_id_type=MESH)

    for k in range(1, n_d):
        pl.semaphore_signal(
            barrier, inc=1, device_id={"tokens": lax.rem(d + k, n_d)}, device_id_type=MESH
        )

    def block(src):
        return pl.ds(pl.multiple_of(src * feats, feats), feats)

    def w_copies(src):
        return [
            pltpu.make_async_copy(wq_hbm.at[block(src)], w.at[block(src), pl.ds(0, qw)], wsem.at[0, src]),
            pltpu.make_async_copy(wk_hbm.at[block(src)], w.at[block(src), pl.ds(qw, HD)], wsem.at[1, src]),
            pltpu.make_async_copy(wv_hbm.at[block(src)], w.at[block(src), pl.ds(qw + HD, HD)], wsem.at[2, src]),
        ]

    x_own = pltpu.make_async_copy(x_hbm, xbuf.at[:, z], xlocal)
    c_own = pltpu.make_async_copy(codes_hbm, codes.at[d], clocal.at[0])
    t_own = pltpu.make_async_copy(trig_hbm, trig.at[d], clocal.at[1])
    c_own.start()
    t_own.start()
    x_own.start()
    for k in range(n_t):
        for copy in w_copies(lax.rem(z + k, n_t)):
            copy.start()

    pl.semaphore_wait(
        barrier, n_d - 1 + has_left.astype(jnp.int32) + has_right.astype(jnp.int32)
    )

    def own_hop(s, side):
        return pltpu.make_async_remote_copy(
            src_ref=x_hbm.at[s], dst_ref=xbuf.at[s, z],
            send_sem=xsend.at[side, s, z], recv_sem=xrecv.at[s, z],
            device_id={"tensor": z + 2 * side - 1}, device_id_type=MESH,
        )

    def hop(s, src, side):
        return pltpu.make_async_remote_copy(
            src_ref=xbuf.at[s, src], dst_ref=xbuf.at[s, src],
            send_sem=xsend.at[side, s, src], recv_sem=xrecv.at[s, src],
            device_id={"tensor": z + 2 * side - 1}, device_id_type=MESH,
        )

    for s in range(subs):
        @pl.when(has_right)
        def _():
            own_hop(s, 1).start()

        @pl.when(has_left)
        def _():
            own_hop(s, 0).start()

    def take(s, k):
        @pl.when(z - k >= 0)
        def _():
            hop(s, z - k, 1).wait_recv()

        @pl.when(z + k < n_t)
        def _():
            hop(s, z + k, 0).wait_recv()

    def forward(s, k):
        @pl.when((z - k >= 0) & has_right)
        def _():
            hop(s, z - k, 1).start()

        @pl.when((z + k < n_t) & has_left)
        def _():
            hop(s, z + k, 0).start()

    def key_copies(k):
        peer = {"tokens": lax.rem(d + k, n_d)}
        return [
            pltpu.make_async_remote_copy(
                src_ref=codes_hbm, dst_ref=codes.at[d],
                send_sem=csend.at[0, k], recv_sem=crecv.at[0, k],
                device_id=peer, device_id_type=MESH,
            ),
            pltpu.make_async_remote_copy(
                src_ref=trig_hbm, dst_ref=trig.at[d],
                send_sem=csend.at[1, k], recv_sem=crecv.at[1, k],
                device_id=peer, device_id_type=MESH,
            ),
        ]

    def dequantize(code):
        value = jnp.zeros(code.shape, jnp.float32)
        for level in range(levels):
            value = jnp.where(code == level, cbt[level:level + 1, :], value)
        return value

    def sub_rows(s):
        return pl.ds(pl.multiple_of(s * tile, tile), tile)

    c_own.wait()
    t_own.wait()
    for s in range(subs):
        mine = pl.ds(s * tile, tile)
        cosine, sine = split_trig(trig[d, mine])
        value = dequantize(codes[d, mine])
        turned = value * cosine + pltpu.roll(value, HD // 2, 1) * sine
        kall[d, mine] = turned.astype(jnp.bfloat16)

    def rot_copy(k):
        return pltpu.make_async_remote_copy(
            src_ref=kall.at[d], dst_ref=kall.at[d],
            send_sem=ksend.at[k], recv_sem=krecv.at[k],
            device_id={"tokens": lax.rem(d + k, n_d)}, device_id_type=MESH,
        )

    for k in range(1, n_d):
        rot_copy(k).start()
    for k in range(1, n_d):
        for copy in key_copies(k):
            copy.start()

    lane = lax.broadcasted_iota(jnp.int32, (8, HD), 1)
    for s in range(subs):
        at = s * tile // HD * HD
        here = jnp.broadcast_to(pos[:, at:at + HD], (8, HD))
        start = s * tile % HD
        spread = here
        for piece in range(HD // tile):
            shift = (piece * tile - start) % HD
            moved = pltpu.roll(here, shift, 1) if shift else here
            spread = jnp.where(lane // tile == piece, moved, spread)
        poss[s] = spread
    bins[...] = jnp.zeros_like(bins)
    outs[...] = jnp.zeros_like(outs)
    acc[...] = jnp.zeros_like(acc)

    for s in range(subs):
        for h in range(heads):
            piece = cot[s * tile:(s + 1) * tile, h * HD:(h + 1) * HD]
            dost[s, h * tile:(h + 1) * tile, :] = piece
        dot_t[s] = dost[s].astype(jnp.float32).T

    def clear(b, carry):
        @pl.when((b < first) | (b >= last))
        def _():
            for s in range(subs):
                probs[s, b] = jnp.zeros((rows, cols), jnp.bfloat16)

        return carry

    lax.fori_loop(0, n_d, clear, 0)

    def add_bins(code, value):
        for level in range(levels):
            chosen = jnp.where(code == level, value, 0.0)
            bins[level] += jnp.sum(chosen.reshape(-1, 8, HD), axis=0)

    def v_copy(s, k):
        mine = vall.at[d, sub_rows(s)]
        return pltpu.make_async_remote_copy(
            src_ref=mine, dst_ref=mine,
            send_sem=vsend.at[s, k], recv_sem=vrecv.at[s, k],
            device_id={"tokens": lax.rem(d + k, n_d)}, device_id_type=MESH,
        )

    def take_values(c):
        for k in range(1, n_d):
            v_copy(c, k).wait_recv()
        part = vall[:, sub_rows(c), :].reshape(n_d * tile, HD)
        vt[c] = part.astype(jnp.float32).T.astype(jnp.bfloat16)

    def add_out(s, c):
        part = probs[s, :, sub_rows(c), :].reshape(n_d * tile, cols)
        outs[s] += jnp.dot(vt[c], part, preferred_element_type=jnp.float32)

    nw = 256 if width % 256 == 0 else HD

    def multiply_all(src):
        def columns(n, carry):
            at = pl.ds(pl.multiple_of(n * nw, nw), nw)
            acc[:, at] += jnp.dot(
                xbuf[:, src].reshape(rows, feats), w[block(src), at],
                preferred_element_type=jnp.float32,
            )
            return carry

        lax.fori_loop(0, width // nw, columns, 0)

    def multiply(s, src):
        acc[sub_rows(s), :] += jnp.dot(
            xbuf[s, src], w[block(src), :], preferred_element_type=jnp.float32
        )

    x_own.wait()

    def near(j, carry):
        src = z + lax.rem(j + 1, 3) - 1

        @pl.when((src >= 0) & (src < n_t))
        def _():
            for copy in w_copies(src):
                copy.wait()

            @pl.when(j == 1)
            def _():
                for s in range(1, subs):
                    hop(s, src, 1).wait_recv()

            @pl.when(j == 2)
            def _():
                for s in range(1, subs):
                    hop(s, src, 0).wait_recv()

            multiply_all(src)

        @pl.when(j == 0)
        def _():
            take(0, 1)
            forward(0, 1)

        return carry

    lax.fori_loop(0, 3, near, 0)
    for k in range(2, n_t):
        for src in (z - k, z + k):
            @pl.when((src >= 0) & (src < n_t))
            def _():
                for copy in w_copies(src):
                    copy.wait()

    def sub(s, carry):
        def step(k, inner):
            take(s, k)
            forward(s, k)

            @pl.when((k == 2) & (s + 1 < subs))
            def _():
                forward(s + 1, 1)

            def side(j, most):
                src = z + k * (2 * j - 1)

                @pl.when((src >= 0) & (src < n_t))
                def _():
                    multiply(s, src)

                return most

            return lax.fori_loop(0, 2, side, inner)

        lax.fori_loop(2, n_t, step, 0)
        mine = sub_rows(s)
        vall[d, mine, :] = acc[mine, qw + HD:qw + 2 * HD].astype(jnp.bfloat16)

        @pl.when(s == 0)
        def _():
            for k in range(1, n_d):
                rot_copy(k).wait_recv()

        for k in range(1, n_d):
            v_copy(s, k).start()
        cosine, sine = split_trig(trig[d, mine])
        for h in range(heads):
            value = acc[mine, h * HD:(h + 1) * HD]
            turned = value * cosine + pltpu.roll(value, HD // 2, 1) * sine
            qst[s, h * tile:(h + 1) * tile, :] = turned.astype(jnp.bfloat16)
        code = codes[d, mine]
        add_bins(code, (levels / total) * (dequantize(code) - acc[mine, qw:qw + HD]))

        column = lax.broadcasted_iota(jnp.int32, (1, HD), 1)
        query = d * rows + s * tile + (column & (tile - 1))
        earliest = query - poss[s, 0:1, :]
        q = qst[s]

        def score(b, peak):
            key = b * rows + lax.broadcasted_iota(jnp.int32, (rows, 1), 0)
            seen = (key <= query) & (key >= earliest)
            value = dot_nt(kall[b], q)
            tops = []
            for g in range(cols // HD):
                at = slice(g * HD, (g + 1) * HD)
                part = jnp.where(seen, value[:, at], NEG_BIG)
                scores[b, :, at] = part
                tops.append(jnp.max(part.reshape(-1, 8, HD), axis=0))
            return jnp.maximum(peak, jnp.concatenate(tops, axis=1))

        peak = lax.fori_loop(first, last, score, jnp.full((8, cols), NEG_BIG, jnp.float32))
        peak = jnp.max(peak, axis=0, keepdims=True)

        def exponent(b, mass):
            value = jnp.exp2((scores[b] - peak) * (scale * math.log2(math.e)))
            scores[b] = value
            return mass + jnp.sum(value.reshape(-1, 8, cols), axis=0)

        mass = lax.fori_loop(first, last, exponent, jnp.zeros((8, cols), jnp.float32))
        inverse = 1.0 / jnp.sum(mass, axis=0, keepdims=True)

        def normal(b, inner):
            probs[s, b] = (scores[b] * inverse).astype(jnp.bfloat16)
            return inner

        lax.fori_loop(first, last, normal, 0)

        @pl.when(s > 0)
        def _():
            take_values(s - 1)

            def older(c, inner):
                add_out(s, c)
                return inner

            def newest(q_at, inner):
                add_out(q_at, s - 1)
                return inner

            lax.fori_loop(0, s, older, 0)
            lax.fori_loop(0, s, newest, 0)

        return carry

    lax.fori_loop(0, subs, sub, 0)
    take_values(subs - 1)

    def close(s, carry):
        add_out(s, subs - 1)
        output = outs[s].astype(jnp.bfloat16).astype(jnp.float32)
        deltas[s] = jnp.broadcast_to(jnp.sum(output * dot_t[s], axis=0, keepdims=True), (8, cols))
        output = output.T.astype(jnp.bfloat16)
        for h in range(heads):
            out_ref[sub_rows(s), h * HD:(h + 1) * HD] = output[h * tile:(h + 1) * tile, :]
        return carry

    lax.fori_loop(0, subs, close, 0)
    for k in range(1, n_d):
        for copy in key_copies(k):
            copy.wait_recv()

    def backward(b, carry):
        grad = jnp.zeros((rows, HD), jnp.float32)
        values = vall[b]
        for s in range(subs):
            dprobs = dot_nt(values, dost[s])
            dscores = (probs[s, b].astype(jnp.float32) * (dprobs - deltas[s, 0:1, :])).astype(jnp.bfloat16)
            grad += jnp.dot(dscores, qst[s], preferred_element_type=jnp.float32)
        grad = grad * scale
        cosine, sine = split_trig(trig[b])
        add_bins(codes[b], grad * cosine - pltpu.roll(grad, HD // 2, 1) * sine)
        return carry

    lax.fori_loop(first, last, backward, 0)
    red[d] = jnp.sum(bins[...], axis=1)

    sums = [
        pltpu.make_async_remote_copy(
            src_ref=red.at[d], dst_ref=red.at[d],
            send_sem=rsend.at[k], recv_sem=rrecv.at[k],
            device_id={"tokens": lax.rem(d + k, n_d)}, device_id_type=MESH,
        )
        for k in range(1, n_d)
    ]
    for copy in sums:
        copy.start()

    def x_drain(s, carry):
        def one(src, inner):
            @pl.when(has_right & (src <= z))
            def _():
                hop(s, src, 1).wait_send()

            @pl.when(has_left & (src >= z))
            def _():
                hop(s, src, 0).wait_send()

            return inner

        lax.fori_loop(0, n_t, one, 0)
        for k in range(1, n_d):
            v_copy(s, k).wait_send()
        return carry

    lax.fori_loop(0, subs, x_drain, 0)
    for k in range(1, n_d):
        rot_copy(k).wait_send()
        for copy in key_copies(k):
            copy.wait_send()
    for copy in sums:
        copy.wait()
    grad_ref[...] = jnp.sum(red[...], axis=0)


def shards(hidden, w_query, w_key, w_value, key_codes, codebook, positions, cotangent):
    rows, feats = hidden.shape
    width = w_query.shape[0]
    heads = w_query.shape[1] // HD
    levels = codebook.shape[1]
    n_t, n_d = lax.axis_size("tensor"), lax.axis_size("tokens")
    subs, tile = SUBS, rows // SUBS
    cols, total = heads * tile, rows * n_d
    trig = trig_table(positions, HD)
    pos = positions.reshape(1, rows)
    anywhere = pl.BlockSpec(memory_space=pl.ANY)
    vmem = pl.BlockSpec(memory_space=pltpu.VMEM)
    dma = pltpu.SemaphoreType.DMA
    bf16, f32 = jnp.bfloat16, jnp.float32
    out, grad = pl.pallas_call(
        functools.partial(kernel, n_t, n_d, heads),
        out_shape=(
            jax.ShapeDtypeStruct((rows, heads * HD), bf16),
            jax.ShapeDtypeStruct((levels, HD), f32),
        ),
        in_specs=[anywhere] * 6 + [vmem] * 3,
        out_specs=(vmem, vmem),
        scratch_shapes=[
            pltpu.VMEM((subs, n_t, tile, feats), bf16),
            pltpu.VMEM((width, heads * HD + 2 * HD), bf16),
            pltpu.VMEM((rows, heads * HD + 2 * HD), f32),
            pltpu.VMEM((n_d, rows, HD), jnp.int32),
            pltpu.VMEM((n_d, rows, HD), f32),
            pltpu.VMEM((n_d, rows, HD), bf16),
            pltpu.VMEM((n_d, rows, HD), bf16),
            pltpu.VMEM((subs, HD, n_d * tile), bf16),
            pltpu.VMEM((subs, cols, HD), bf16),
            pltpu.VMEM((subs, cols, HD), bf16),
            pltpu.VMEM((subs, HD, cols), f32),
            pltpu.VMEM((subs, n_d, rows, cols), bf16),
            pltpu.VMEM((n_d, rows, cols), f32),
            pltpu.VMEM((subs, 8, cols), f32),
            pltpu.VMEM((levels, 8, HD), f32),
            pltpu.VMEM((n_d, levels, HD), f32),
            pltpu.VMEM((subs, 8, HD), jnp.int32),
            pltpu.VMEM((subs, HD, cols), f32),
            dma((2, subs, n_t)),
            dma((subs, n_t)),
            dma,
            dma((3, n_t)),
            dma((2, n_d)),
            dma((2, n_d)),
            dma((2,)),
            dma((n_d,)),
            dma((n_d,)),
            dma((subs, n_d)),
            dma((subs, n_d)),
            dma((n_d,)),
            dma((n_d,)),
        ],
        compiler_params=pltpu.CompilerParams(
            collective_id=0, has_side_effects=True, vmem_limit_bytes=67043328
        ),
    )(
        hidden.reshape(subs, tile, feats), w_query, w_key, w_value,
        key_codes, trig, codebook.T, pos, cotangent,
    )
    return out, grad.T


def solution(mesh):
    placed = (
        P("tokens", "tensor"),
        P(None, "tensor"),
        P(None, "tensor"),
        P(None, "tensor"),
        P("tokens", "tensor"),
        P("tensor", None),
        P("tokens"),
        P("tokens", "tensor"),
    )
    return jax.shard_map(
        shards,
        mesh=mesh,
        in_specs=placed,
        out_specs=(P("tokens", "tensor"), P("tensor", None)),
        check_vma=False,
    )
```

time: 110 us -> 103 us (0.936)
  Pallas kernels: 104 us -> 97 us
    pallas_call x1, Pallas kernels: 104 us -> 97 us  [shards(): pl.pallas_call(functools.partial(kernel, n_t, n_d, heads), out_shape=(jax...]
where the time goes in v1:
time: 103 us
  Pallas kernels  97 us (94%)
  local copies, waits for them, and re-layouts  3.25 us (3%)
  other arithmetic  1.89 us (2%)
    pallas_call x1, Pallas kernels, shards(): pl.pallas_call(functools.partial(kernel, n_t, n_d, heads), out_shape=(jax...  97 us
    unnamed x2, local copies, waits for them, and re-layouts  3.16 us

profile of v1, /device:TPU:0, one launch (start us, length us, event | category | flops | bytes accessed | tf_op | source)
XLA Modules:
  0.0 102.8 jit_solution(15784551589335039165)
XLA Ops:
  0.7 0.1 mul.28
  0.7 0.7 convert_element_type.10
  1.4 1.2 %fusion.trig_hbm = f32[256,128]{1,0:T(8,128)} fusion(f32[128]{0:T(128)S(1)} %mul.28, f32[256]{0:T(256)S(1)} %convert_element_type.10, pred[128]{0:T(512)(128)(4,1)S(1)} %iota_compare_fusion), kind=kLoop, calls=%fused_computation.2 | loop fusion | flops 65536 | bytes 132736 | tf_op jit(solution)/shard_map/jit(_where)/select_n | solution.py:23
  2.6 97.0 %shard_map.95 = (bf16[256,1024]{1,0:T(8,128)(2,1)}, f32[16,128]{1,0:T(8,128)}) custom-call(bf16[4,64,2048]{2,1,0:T(8,128)(2,1)} %bitcast.4, bf16[8192,1024]{1,0:T(8,128)(2,1)} %wq_hbm.1, bf16[8192,128]{1,0:T(8,128)(2,1)} %wk_hbm.1, bf16[8192,128]{1,0:T(8,128)(2,1)} %wv_hbm.1, s32[256,128]{1,0:T(8,128)} %codes_hbm.1, f32[256,128]{1,0:T(8,128)} %fusion.trig_hbm, ...), custom_call_target="tpu_custom_call" | custom-call | tf_op jit(solution)/shard_map/pallas_call | solution.py:467
  99.6 1.9 %copy.12 = bf16[256,1024]{1,0:T(8,128)(2,1)} copy(bf16[256,1024]{1,0:T(8,128)(2,1)} %get-tuple-element.8) | data formatting | bytes 1048576
  101.5 1.3 %copy.13 = f32[128,16]{0,1:T(8,128)} copy(f32[128,16]{0,1:T(8,128)} %bitcast.6) | data formatting | bytes 16384
  (3 shorter events, 0.0 us)
